TPU v7x, 32 devices: a whole 2x2x4 slice. The times are simulated.
32 devices in a mesh: row: 8 (over y, x, core), col: 4 (over z).
Axes of the slice: x: 2, y: 2, z: 4, core: 2. Of those that a mesh axis runs over, the one named last changes fastest.
Arguments:
- documents: float32 [6144, 768], P('row', 'col'), may hold values from -6 to 6
- projection: float32 [768, 768], P('col'), may hold values from -0.21875 to 0.21875
- landmarks: float32 [16384, 768], P('col', 'row'), may hold values from -6 to 6
- coefficients: float32 [16384, 128], P('col'), may hold values from -6 to 6
- inverse_tiles: float32 [16384, 16384], P('col', 'row'), may hold values from -0.046875 to 0.046875
- labels: int32 [6144, 128], P('row'), may hold values 0 or 1
Outputs:
- new_coefficients: float32 [16384, 128], P('col')
- residual: float32 [6144, 128], P('row')
All inputs are finite; a program needn't handle non-finite values. No bound on the sum of `labels` on one device may be relied on, other than what follows from the above.
Results may differ from a plain program's by a relative error of at most 0.0001.
Values sent between devices are 32-bit elements; how exact they have to be, the bound alone decides.
A program may use at most 128 MiB of HBM per device.

v0:
```python
import jax
import jax.numpy as jnp
from jax import lax
from jax.sharding import PartitionSpec as P

ITERS = 2


def broadcast(block, axis, owner):
    block = jnp.where(lax.axis_index(axis) == owner, block, jnp.zeros_like(block))
    return lax.psum(block, axis)


def on_device(documents, projection, landmarks, coefficients, inverse_tiles, labels):
    highest = lax.Precision.HIGHEST
    land_full = lax.all_gather(landmarks, "row", axis=1, tiled=True)
    sq_land = jnp.sum(land_full * land_full, axis=1)
    feature_width = land_full.shape[1]
    proj_share = lax.psum_scatter(
        jnp.dot(documents, projection, precision=highest, preferred_element_type=jnp.float32),
        "col",
        scatter_dimension=0,
        tiled=True,
    )
    rows_in = lax.all_gather(proj_share, "col", axis=0, tiled=True)
    sq_doc = jnp.sum(rows_in * rows_in, axis=1)
    inner = lax.dot_general(
        rows_in,
        land_full,
        (((1,), (1,)), ((), ())),
        precision=highest,
        preferred_element_type=jnp.float32,
    )
    kernel = jnp.exp(-2.0 * (sq_doc[:, None] + sq_land[None, :] - 2.0 * inner) / feature_width)
    row_count = lax.axis_size("row")
    col_count = lax.axis_size("col")
    step_size = 64.0 / (documents.shape[0] * row_count)
    block_rows = inverse_tiles.shape[1]
    group_size = row_count // col_count
    row_index = lax.axis_index("row")
    source = row_index // group_size
    offset = row_index % group_size * block_rows
    current = coefficients
    target = labels.astype(jnp.float32)
    residual = jnp.zeros((documents.shape[0], labels.shape[1]), jnp.float32)
    for iteration in range(ITERS):
        local_pred = jnp.dot(kernel, current, precision=highest, preferred_element_type=jnp.float32)
        predicted = lax.psum(local_pred, "col")
        residual = jax.nn.sigmoid(predicted) - target
        local_grad = lax.dot_general(
            kernel,
            residual,
            (((0,), (0,)), ((), ())),
            precision=highest,
            preferred_element_type=jnp.float32,
        )
        gradient = lax.psum(local_grad, "row")
        grad_block = lax.dynamic_slice_in_dim(gradient, offset, block_rows, 0)
        grad_block = broadcast(grad_block, "col", source)
        product_term = jnp.dot(
            inverse_tiles, grad_block, precision=highest, preferred_element_type=jnp.float32
        )
        current = current - step_size * lax.psum(product_term, "row")
    return (current, residual)


def solution(mesh):
    in_specs = (
        P("row", "col"),
        P("col", None),
        P("col", "row"),
        P("col", None),
        P("col", "row"),
        P("row", None),
    )
    out_specs = (P("col", None), P("row", None))
    return jax.shard_map(
        on_device, mesh=mesh, in_specs=in_specs, out_specs=out_specs, check_vma=False
    )
```

profile of v0, /device:TPU:0, one launch (start us, length us, event | category | flops | bytes accessed | tf_op | source)
XLA Modules:
  0.0 830.2 jit_solution(13493316278043722178)
XLA Ops:
  7.2 0.0 reduce-scatter.2.cloned.1.call-start
  7.2 1.0 copy-done
  8.2 4.6 fusion.11
  12.8 0.0 all-gather.3.cloned.1.call-start
  12.9 50.5 %reduce-scatter.2.cloned.1.call-done = f32[192,768]{1,0:T(8,128)} async-done(((f32[768,768]{1,0:T(8,128)}), f32[192,768]{1,0:T(8,128)}) %reduce-scatter.2.cloned.1.call-update) | async-done | bytes 589840 | tf_op jit(solution)/shard_map/reduce_scatter | solution.py:19
  63.4 0.0 all-gather.5.cloned.1.call-start
  63.5 0.7 all-gather.5.cloned.1.call-update
  64.2 0.0 all-reduce.9.cloned.1.call-start
  64.2 50.2 %all-gather.3.cloned.1.call-done = f32[768,768]{1,0:T(8,128)} async-done(((f32[192,768]{1,0:T(8,128)}), f32[768,768]{1,0:T(8,128)}) %all-gather.3.cloned.1.call-update) | async-done | bytes 2359312 | tf_op jit(solution)/shard_map/all_gather | solution.py:25
  114.4 2.0 multiply_reduce_fusion.1
  116.4 70.6 %all-gather.5.cloned.1.call-done = f32[4096,768]{0,1:T(8,128)} async-done(((f32[4096,96]{0,1:T(8,128)}), f32[4096,768]{0,1:T(8,128)}) %all-gather.5.cloned.1.call-update) | async-done | bytes 12582928 | tf_op jit(solution)/shard_map/all_gather | solution.py:16
  187.1 5.9 multiply_reduce_fusion
  192.9 2.3 copy-done.3
  195.2 32.1 %multiply_exponential_fusion = f32[768,4096]{1,0:T(8,128)S(1)} fusion(f32[768,768]{1,0:T(8,128)S(1)} %copy-done.5, f32[4096,768]{0,1:T(8,128)S(1)} %copy-done.3, f32[4096]{0:T(1024)S(1)} %multiply_reduce_fusion, f32[768]{0:T(1024)S(1)} %multiply_reduce_fusion.1), kind=kOutput, calls=%fused_computation | convolution fusion | flops 29003612160 | bytes 27544576 | tf_op jit(solution)/shard_map/dot_general | solution.py:27
  227.4 4.5 copy-done.2
  231.9 10.6 %fusion.12 = f32[768,128]{1,0:T(8,128)} fusion(f32[768,4096]{1,0:T(8,128)S(1)} %multiply_exponential_fusion, f32[4096,128]{1,0:T(8,128)S(1)} %copy-done.4), kind=kOutput, calls=%fused_computation.22 | convolution fusion | flops 4831838208 | bytes 15073280 | tf_op jit(solution)/shard_map/dot_general | solution.py:47
  242.6 0.0 all-reduce.11.cloned.1.call-start
  242.6 37.0 %all-reduce.9.cloned.1.call-done = f32[768,128]{1,0:T(8,128)} async-done(((f32[768,128]{1,0:T(8,128)}), f32[768,128]{1,0:T(8,128)}) %all-reduce.9.cloned.1.call-update) | async-done | bytes 393232 | tf_op jit(solution)/shard_map/psum | solution.py:48
  279.7 24.0 %fusion.1 = f32[4096,128]{1,0:T(8,128)} fusion(f32[768,4096]{1,0:T(8,128)} %copy-done.2, s32[768,128]{1,0:T(8,128)S(1)} %copy-done.6, f32[768,128]{1,0:T(8,128)} %all-reduce.9.cloned.1.call-done), kind=kOutput, calls=%fused_computation.11 | convolution fusion | flops 4832329728 | bytes 15466496 | tf_op jit(solution)/shard_map/dot_general | solution.py:50
  303.7 0.0 all-reduce.11.cloned.1.call-update
  303.7 0.0 all-reduce.13.cloned.1.call-start
  303.8 61.6 %all-reduce.11.cloned.1.call-done = f32[4096,128]{1,0:T(8,128)} async-done(((f32[4096,128]{1,0:T(8,128)}), f32[4096,128]{1,0:T(8,128)}) %all-reduce.11.cloned.1.call-update) | async-done | bytes 2097168 | tf_op jit(solution)/shard_map/psum | solution.py:57
  365.4 2.3 dynamic-slice_select_fusion.1
  367.6 0.0 all-reduce.15.cloned.1.call-start
  367.7 51.5 %all-reduce.13.cloned.1.call-done = f32[2048,128]{1,0:T(8,128)} async-done(((f32[2048,128]{1,0:T(8,128)}), f32[2048,128]{1,0:T(8,128)}) %all-reduce.13.cloned.1.call-update) | async-done | bytes 1048592 | tf_op jit(solution)/shard_map/psum | solution.py:11
  419.1 42.4 %convolution_bitcast_fusion.1 = f32[4096,128]{0,1:T(8,128)} fusion(f32[2048,128]{1,0:T(8,128)} %all-reduce.13.cloned.1.call-done, f32[4096,2048]{1,0:T(8,128)} %param.10), kind=kOutput, calls=%fused_computation.3 | convolution fusion | flops 12884901888 | bytes 36700160 | tf_op jit(solution)/shard_map/dot_general | solution.py:60
  461.6 0.0 all-reduce.15.cloned.1.call-update
  461.6 0.0 all-reduce.17.cloned.1.call-start
  461.7 1.9 copy.8
  463.6 59.2 %all-reduce.15.cloned.1.call-done = f32[4096,128]{0,1:T(8,128)} async-done(((f32[4096,128]{0,1:T(8,128)}), f32[4096,128]{0,1:T(8,128)}) %all-reduce.15.cloned.1.call-update) | async-done | bytes 2097168 | tf_op jit(solution)/shard_map/psum | solution.py:63
  522.8 13.9 %fusion = f32[768,128]{1,0:T(8,128)} fusion(f32[768,4096]{1,0:T(8,128)} %copy-done.2, f32[4096,128]{0,1:T(8,128)S(1)} %copy.8, f32[4096,128]{0,1:T(8,128)} %all-reduce.15.cloned.1.call-done), kind=kOutput, calls=%fused_computation.9 | convolution fusion | flops 4832886784 | bytes 17170432 | tf_op jit(solution)/shard_map/dot_general | solution.py:47
  536.7 0.0 all-reduce.17.cloned.1.call-update
  536.7 0.0 all-reduce.19.cloned.1.call-start
  536.7 36.1 %all-reduce.17.cloned.1.call-done = f32[768,128]{1,0:T(8,128)} async-done(((f32[768,128]{1,0:T(8,128)}), f32[768,128]{1,0:T(8,128)}) %all-reduce.17.cloned.1.call-update) | async-done | bytes 393232 | tf_op jit(solution)/shard_map/psum | solution.py:48
  572.9 1.1 divide_subtract_fusion
  574.0 23.8 %fusion.13 = f32[4096,128]{1,0:T(8,128)} fusion(f32[768,4096]{1,0:T(8,128)} %copy-done.2, f32[768,128]{1,0:T(8,128)S(1)} %divide_subtract_fusion), kind=kOutput, calls=%fused_computation.23 | convolution fusion | flops 4831838208 | bytes 15073280 | tf_op jit(solution)/shard_map/dot_general | solution.py:50
  597.8 0.0 all-reduce.19.cloned.1.call-update
  597.8 0.0 all-reduce.21.cloned.1.call-start
  597.9 61.6 %all-reduce.19.cloned.1.call-done = f32[4096,128]{1,0:T(8,128)} async-done(((f32[4096,128]{1,0:T(8,128)}), f32[4096,128]{1,0:T(8,128)}) %all-reduce.19.cloned.1.call-update) | async-done | bytes 2097168 | tf_op jit(solution)/shard_map/psum | solution.py:57
  659.5 2.3 dynamic-slice_select_fusion
  661.8 0.0 all-reduce.21.cloned.1.call-update
  661.8 0.0 all-reduce.23.cloned.1.call-start
  661.9 51.4 %all-reduce.21.cloned.1.call-done = f32[2048,128]{1,0:T(8,128)} async-done(((f32[2048,128]{1,0:T(8,128)}), f32[2048,128]{1,0:T(8,128)}) %all-reduce.21.cloned.1.call-update) | async-done | bytes 1048592 | tf_op jit(solution)/shard_map/psum | solution.py:11
  713.3 42.0 %convolution_bitcast_fusion = f32[4096,128]{0,1:T(8,128)} fusion(f32[2048,128]{1,0:T(8,128)} %all-reduce.21.cloned.1.call-done, f32[4096,2048]{1,0:T(8,128)} %param.10), kind=kOutput, calls=%fused_computation.2 | convolution fusion | flops 12884901888 | bytes 36700160 | tf_op jit(solution)/shard_map/dot_general | solution.py:60
  755.3 0.0 all-reduce.23.cloned.1.call-update
  755.4 61.2 %all-reduce.23.cloned.1.call-done = f32[4096,128]{0,1:T(8,128)} async-done(((f32[4096,128]{0,1:T(8,128)}), f32[4096,128]{0,1:T(8,128)}) %all-reduce.23.cloned.1.call-update) | async-done | bytes 2097168 | tf_op jit(solution)/shard_map/psum | solution.py:63
  816.5 4.0 multiply_subtract_fusion
  820.6 2.9 copy.9
  (17 shorter events, 0.1 us)
Async XLA Ops:
  7.2 1.1 copy-start
  7.2 56.2 %reduce-scatter.2.cloned.1.call-start = ((), (), s32[]{:S(2)}) async-start(), calls=%async_computation.1 | async-start | bytes 2949120 | tf_op jit(solution)/shard_map/reduce_scatter | solution.py:19
  12.8 101.5 %all-gather.3.cloned.1.call-start = ((), (), s32[]{:S(2)}) async-start(), calls=%async_computation.2 | async-start | bytes 2949120 | tf_op jit(solution)/shard_map/all_gather | solution.py:25
  63.4 123.6 %all-gather.5.cloned.1.call-start = ((), (), s32[]{:S(2)}) async-start(), calls=%async_computation.3 | async-start | bytes 14155776 | tf_op jit(solution)/shard_map/all_gather | solution.py:16
  64.2 215.5 %all-reduce.9.cloned.1.call-start = ((), (), s32[]{:S(2)}) async-start(), calls=%async_computation.4 | async-start | bytes 786432 | tf_op jit(solution)/shard_map/psum | solution.py:48
  114.4 78.6 %copy-start.5 = (f32[768,768]{1,0:T(8,128)S(1)}, f32[768,768]{1,0:T(8,128)}, u32[]{:S(2)}) copy-start(f32[768,768]{1,0:T(8,128)} %all-gather.3.cloned.1.call-done) | copy-start | bytes 7077892
  187.1 8.2 copy-start.3
  195.2 36.7 %copy-start.4 = (f32[4096,128]{1,0:T(8,128)S(1)}, f32[4096,128]{1,0:T(8,128)}, u32[]{:S(2)}) copy-start(f32[4096,128]{1,0:T(8,128)} %param.9) | copy-start | bytes 6291460
  227.4 4.5 copy-start.2
  231.9 47.8 %copy-start.6 = (s32[768,128]{1,0:T(8,128)S(1)}, s32[768,128]{1,0:T(8,128)}, u32[]{:S(2)}) copy-start(s32[768,128]{1,0:T(8,128)} %param.11) | copy-start | bytes 1179652
  242.6 122.8 %all-reduce.11.cloned.1.call-start = ((), (), s32[]{:S(2)}) async-start(), calls=%async_computation.5 | async-start | bytes 4194304 | tf_op jit(solution)/shard_map/psum | solution.py:57
  303.7 115.4 %all-reduce.13.cloned.1.call-start = ((), (), s32[]{:S(2)}) async-start(), calls=%async_computation.6 | async-start | bytes 2097152 | tf_op jit(solution)/shard_map/psum | solution.py:11
  367.6 155.1 %all-reduce.15.cloned.1.call-start = ((), (), s32[]{:S(2)}) async-start(), calls=%async_computation.7 | async-start | bytes 4194304 | tf_op jit(solution)/shard_map/psum | solution.py:63
  461.6 111.3 %all-reduce.17.cloned.1.call-start = ((), (), s32[]{:S(2)}) async-start(), calls=%async_computation.8 | async-start | bytes 786432 | tf_op jit(solution)/shard_map/psum | solution.py:48
  536.7 122.8 %all-reduce.19.cloned.1.call-start = ((), (), s32[]{:S(2)}) async-start(), calls=%async_computation.9 | async-start | bytes 4194304 | tf_op jit(solution)/shard_map/psum | solution.py:57
  574.0 23.8 %copy-start.7 = (f32[768,128]{1,0:T(8,128)}, f32[768,128]{1,0:T(8,128)S(1)}, u32[]{:S(2)}) copy-start(f32[768,128]{1,0:T(8,128)S(1)} %divide_subtract_fusion) | copy-start | bytes 1179652
  597.8 115.5 %all-reduce.21.cloned.1.call-start = ((), (), s32[]{:S(2)}) async-start(), calls=%async_computation.10 | async-start | bytes 2097152 | tf_op jit(solution)/shard_map/psum | solution.py:11
  661.8 154.7 %all-reduce.23.cloned.1.call-start = ((), (), s32[]{:S(2)}) async-start(), calls=%async_computation.11 | async-start | bytes 4194304 | tf_op jit(solution)/shard_map/psum | solution.py:63
  816.5 6.9 copy-start.1
Sparse Core Ops, SparseCore 0:
  13.0 50.4 reduce-scatter.1
  65.0 49.3 all-gather.2
  116.3 70.7 all-gather.4
  242.7 36.9 all-reduce.8
  303.8 61.4 all-reduce.10
  368.2 50.9 all-reduce.12
  461.7 61.0 all-reduce.14
  536.8 36.0 all-reduce.16
  597.9 61.5 all-reduce.18
  662.3 50.9 all-reduce.20
  755.5 61.0 all-reduce.22
where the time goes:
time: 834 us; the launch traced here: 830 us
  waiting for transfers between devices  592 us (71%)
  matrix products  194 us (23%)
  other arithmetic  17.6 us (2%)
  between operations  14.2 us (2%)
  local copies, waits for them, and re-layouts  12.6 us (2%)
    psum x2, waiting for transfers between devices, on_device(): gradient = lax.psum(local_grad, 'row')  123 us
    psum x2, waiting for transfers between devices, on_device(): current = current - step_size * lax.psum(product_term, 'row')  120 us
    psum x2, waiting for transfers between devices, broadcast(): return lax.psum(block, axis)  103 us
    dot_general x2, matrix products, on_device(): jnp.dot(inverse_tiles, grad_block, precision=highest, preferred_element_t...  84.5 us
    psum x2, waiting for transfers between devices, on_device(): predicted = lax.psum(local_pred, 'col')  73.2 us
    all_gather x1, waiting for transfers between devices, on_device(): land_full = lax.all_gather(landmarks, 'row', axis=1, tiled=True)  70.6 us
    reduce_scatter x1, waiting for transfers between devices, on_device(): lax.psum_scatter(jnp.dot(documents, projection, precision=highest, prefer...  50.5 us
    all_gather x1, waiting for transfers between devices, on_device(): rows_in = lax.all_gather(proj_share, 'col', axis=0, tiled=True)  50.2 us
  transfers between devices with their start and end apart: 11, of which 11 were waited for; matrix products, arithmetic and copies ran while one was open for 0% of the time, Pallas kernels for 0%

commit v1 on v0

--- a/solution.py
+++ b/solution.py
@@ -13,7 +13,21 @@
 
 def on_device(documents, projection, landmarks, coefficients, inverse_tiles, labels):
     highest = lax.Precision.HIGHEST
-    land_full = lax.all_gather(landmarks, "row", axis=1, tiled=True)
+    ways, here, step = (lax.axis_size("row"), lax.axis_index("row"), landmarks.shape[1])
+    lengths = [n * ways if d == 1 else n for d, n in enumerate(landmarks.shape)]
+    full = lax.dynamic_update_slice_in_dim(
+        jnp.zeros(lengths, landmarks.dtype), landmarks, here * step, axis=1
+    )
+    going_up = going_down = landmarks
+    for far in range(1, ways // 2 + 1):
+        going_up = lax.ppermute(going_up, "row", [(d, (d + 1) % ways) for d in range(ways)])
+        full = lax.dynamic_update_slice_in_dim(full, going_up, (here - far) % ways * step, axis=1)
+        if 2 * far < ways:
+            going_down = lax.ppermute(going_down, "row", [(d, (d - 1) % ways) for d in range(ways)])
+            full = lax.dynamic_update_slice_in_dim(
+                full, going_down, (here + far) % ways * step, axis=1
+            )
+    land_full = full
     sq_land = jnp.sum(land_full * land_full, axis=1)
     feature_width = land_full.shape[1]
     proj_share = lax.psum_scatter(

time: 834 us -> 795 us (0.953)
  waiting for transfers between devices: 592 us -> 518 us
  local copies, waits for them, and re-layouts: 12.6 us -> 34 us
  starting transfers between devices: 0.45 us -> 10.4 us
    ppermute x0 -> x7, waiting for transfers between devices: none -> 93.2 us  [the longest x4 83.9 us: on_device(): lax.ppermute(going_up, 'row', [(d, (d + 1) % ways) for d in range(ways)])]
    all_gather x1 -> x0, waiting for transfers between devices: 70.6 us -> none  [on_device(): land_full = lax.all_gather(landmarks, 'row', axis=1, tiled=True)]
    reduce_scatter x1, waiting for transfers between devices: 50.5 us -> 0.01 us  [on_device(): lax.psum_scatter(jnp.dot(documents, projection, precision=highest, prefer...]
    all_gather x1, waiting for transfers between devices: 50.2 us -> 2.19 us  [on_device(): rows_in = lax.all_gather(proj_share, 'col', axis=0, tiled=True)]
    dynamic_update_slice x0 -> x8, local copies, waits for them, and re-layouts: none -> 17.3 us  [the longest x4 9.39 us: on_device(): lax.dynamic_update_slice_in_dim(full, going_up, (here - far) % ways * ste...]
    ppermute x0 -> x7, starting transfers between devices: none -> 10 us  [the longest x3 8.48 us: on_device(): lax.ppermute(going_down, 'row', [(d, (d - 1) % ways) for d in range(ways)])]
  transfers between devices with their start and end apart: 11 -> 17, of which waited for: 11 -> 15; matrix products, arithmetic and copies ran while one was open for 0% -> 4% of each run, Pallas kernels for 0% -> 0%
where the time goes in v1:
time: 795 us; the launch traced here: 790 us
  waiting for transfers between devices  518 us (65%)
  matrix products  196 us (25%)
  local copies, waits for them, and re-layouts  34 us (4%)
  other arithmetic  17.4 us (2%)
  between operations  14.5 us (2%)
  starting transfers between devices  10.4 us (1%)
    psum x2, waiting for transfers between devices, on_device(): gradient = lax.psum(local_grad, 'row')  123 us
    psum x2, waiting for transfers between devices, on_device(): current = current - step_size * lax.psum(product_term, 'row')  120 us
    psum x2, waiting for transfers between devices, broadcast(): return lax.psum(block, axis)  103 us
    dot_general x2, matrix products, on_device(): jnp.dot(inverse_tiles, grad_block, precision=highest, preferred_element_t...  84.6 us
    ppermute x4, waiting for transfers between devices, on_device(): lax.ppermute(going_up, 'row', [(d, (d + 1) % ways) for d in range(ways)])  83.9 us
    psum x2, waiting for transfers between devices, on_device(): predicted = lax.psum(local_pred, 'col')  76.1 us
    dot_general x2, matrix products, on_device(): lax.dot_general(kernel, residual, (((0,), (0,)), ((), ())), precision=hig...  47.7 us
    dot_general x1, matrix products, on_device(): lax.dot_general(rows_in, land_full, (((1,), (1,)), ((), ())), precision=h...  34.6 us
  transfers between devices with their start and end apart: 17, of which 15 were waited for; matrix products, arithmetic and copies ran while one was open for 4% of the time, Pallas kernels for 0%

profile of v1, /device:TPU:0, one launch (start us, length us, event | category | flops | bytes accessed | tf_op | source)
XLA Modules:
  0.0 790.4 jit_solution(3696590498064333917)
XLA Ops:
  7.2 1.0 copy-done
  8.2 4.5 fusion.11
  12.9 0.5 collective-permute-start
  13.4 2.9 collective-permute-start.1
  16.4 32.3 %collective-permute-done = f32[4096,96]{0,1:T(8,128)S(1)} collective-permute-done((f32[4096,96]{0,1:T(8,128)S(1)}, f32[4096,96]{0,1:T(8,128)S(1)}, u32[]{:S(2)}, u32[]{:S(2)}) %collective-permute-start) | collective-permute-done | bytes 1572896 | tf_op jit(solution)/shard_map/ppermute | solution.py:23
  48.7 0.5 collective-permute-start.2
  49.2 0.9 collective-permute-done.1
  50.1 2.9 collective-permute-start.3
  53.0 30.6 %collective-permute-done.2 = f32[4096,96]{0,1:T(8,128)} collective-permute-done((f32[4096,96]{0,1:T(8,128)S(1)}, f32[4096,96]{0,1:T(8,128)}, u32[]{:S(2)}, u32[]{:S(2)}) %collective-permute-start.2) | collective-permute-done | bytes 1572896 | tf_op jit(solution)/shard_map/ppermute | solution.py:23
  83.6 6.1 broadcast_in_dim.2
  89.7 1.3 constant_dynamic-update-slice_fusion.7
  91.0 2.7 constant_dynamic-update-slice_fusion.6
  93.7 2.6 collective-permute-start.5
  96.3 2.7 constant_dynamic-update-slice_fusion.5
  99.0 11.7 %collective-permute-done.4 = f32[4096,96]{0,1:T(8,128)} collective-permute-done((f32[4096,96]{0,1:T(8,128)}, f32[4096,96]{0,1:T(8,128)}, u32[]{:S(2)}, u32[]{:S(2)}) %collective-permute-start.4) | collective-permute-done | bytes 1572896 | tf_op jit(solution)/shard_map/ppermute | solution.py:23
  110.7 0.4 collective-permute-start.6
  111.2 2.7 constant_dynamic-update-slice_fusion.4
  113.8 2.7 constant_dynamic-update-slice_fusion.3
  116.5 2.8 constant_dynamic-update-slice_fusion.2
  119.3 8.4 %collective-permute-done.5 = f32[4096,96]{0,1:T(8,128)S(1)} collective-permute-done((f32[4096,96]{0,1:T(8,128)}, f32[4096,96]{0,1:T(8,128)S(1)}, u32[]{:S(2)}, u32[]{:S(2)}) %collective-permute-start.5) | collective-permute-done | bytes 1572896 | tf_op jit(solution)/shard_map/ppermute | solution.py:26
  127.7 1.3 constant_dynamic-update-slice_fusion.1
  129.0 9.3 %collective-permute-done.6 = f32[4096,96]{0,1:T(8,128)S(1)} collective-permute-done((f32[4096,96]{0,1:T(8,128)}, f32[4096,96]{0,1:T(8,128)S(1)}, u32[]{:S(2)}, u32[]{:S(2)}) %collective-permute-start.6) | collective-permute-done | bytes 1572896 | tf_op jit(solution)/shard_map/ppermute | solution.py:23
  138.2 1.2 constant_dynamic-update-slice_fusion
  139.5 5.7 multiply_reduce_fusion
  145.2 2.2 all-gather.2.cloned.1.call-done
  147.4 2.0 multiply_reduce_fusion.1
  149.8 34.6 %multiply_exponential_fusion = f32[768,4096]{1,0:T(8,128)S(1)} fusion(f32[768,768]{1,0:T(8,128)S(1)} %copy-done.4, f32[4096,768]{0,1:T(8,128)} %constant_dynamic-update-slice_fusion, f32[4096]{0:T(1024)S(1)} %multiply_reduce_fusion, f32[768]{0:T(1024)S(1)} %multiply_reduce_fusion.1), kind=kOutput, calls=%fused_computation | convolution fusion | flops 29003612160 | bytes 27544576 | tf_op jit(solution)/shard_map/dot_general | solution.py:41
  184.3 4.5 copy-done.2
  188.8 10.6 %fusion.12 = f32[768,128]{1,0:T(8,128)} fusion(f32[768,4096]{1,0:T(8,128)S(1)} %multiply_exponential_fusion, f32[4096,128]{1,0:T(8,128)S(1)} %copy-done.3), kind=kOutput, calls=%fused_computation.30 | convolution fusion | flops 4831838208 | bytes 15073280 | tf_op jit(solution)/shard_map/dot_general | solution.py:61
  199.6 40.0 %all-reduce.9.cloned.1.call-done = f32[768,128]{1,0:T(8,128)} async-done(((f32[768,128]{1,0:T(8,128)}), f32[768,128]{1,0:T(8,128)}) %all-reduce.9.cloned.1.call-update) | async-done | bytes 393232 | tf_op jit(solution)/shard_map/psum | solution.py:62
  239.5 23.9 %fusion.1 = f32[4096,128]{1,0:T(8,128)} fusion(f32[768,4096]{1,0:T(8,128)} %copy-done.2, s32[768,128]{1,0:T(8,128)S(1)} %copy-done.7, f32[768,128]{1,0:T(8,128)} %all-reduce.9.cloned.1.call-done), kind=kOutput, calls=%fused_computation.11 | convolution fusion | flops 4832329728 | bytes 15466496 | tf_op jit(solution)/shard_map/dot_general | solution.py:64
  263.5 61.6 %all-reduce.11.cloned.1.call-done = f32[4096,128]{1,0:T(8,128)} async-done(((f32[4096,128]{1,0:T(8,128)}), f32[4096,128]{1,0:T(8,128)}) %all-reduce.11.cloned.1.call-update) | async-done | bytes 2097168 | tf_op jit(solution)/shard_map/psum | solution.py:71
  325.0 2.3 dynamic-slice_select_fusion.1
  327.4 51.4 %all-reduce.13.cloned.1.call-done = f32[2048,128]{1,0:T(8,128)} async-done(((f32[2048,128]{1,0:T(8,128)}), f32[2048,128]{1,0:T(8,128)}) %all-reduce.13.cloned.1.call-update) | async-done | bytes 1048592 | tf_op jit(solution)/shard_map/psum | solution.py:11
  378.8 42.5 %convolution_bitcast_fusion.1 = f32[4096,128]{0,1:T(8,128)} fusion(f32[2048,128]{1,0:T(8,128)} %all-reduce.13.cloned.1.call-done, f32[4096,2048]{1,0:T(8,128)} %param.10), kind=kOutput, calls=%fused_computation.3 | convolution fusion | flops 12884901888 | bytes 36700160 | tf_op jit(solution)/shard_map/dot_general | solution.py:74
  421.4 1.9 copy.8
  423.3 59.2 %all-reduce.15.cloned.1.call-done = f32[4096,128]{0,1:T(8,128)} async-done(((f32[4096,128]{0,1:T(8,128)}), f32[4096,128]{0,1:T(8,128)}) %all-reduce.15.cloned.1.call-update) | async-done | bytes 2097168 | tf_op jit(solution)/shard_map/psum | solution.py:77
  482.5 13.9 %fusion = f32[768,128]{1,0:T(8,128)} fusion(f32[768,4096]{1,0:T(8,128)} %copy-done.2, f32[4096,128]{0,1:T(8,128)S(1)} %copy.8, f32[4096,128]{0,1:T(8,128)} %all-reduce.15.cloned.1.call-done), kind=kOutput, calls=%fused_computation.9 | convolution fusion | flops 4832886784 | bytes 17170432 | tf_op jit(solution)/shard_map/dot_general | solution.py:61
  496.5 36.1 %all-reduce.17.cloned.1.call-done = f32[768,128]{1,0:T(8,128)} async-done(((f32[768,128]{1,0:T(8,128)}), f32[768,128]{1,0:T(8,128)}) %all-reduce.17.cloned.1.call-update) | async-done | bytes 393232 | tf_op jit(solution)/shard_map/psum | solution.py:62
  532.6 1.1 divide_subtract_fusion
  533.7 23.8 %fusion.13 = f32[4096,128]{1,0:T(8,128)} fusion(f32[768,4096]{1,0:T(8,128)} %copy-done.2, f32[768,128]{1,0:T(8,128)S(1)} %divide_subtract_fusion), kind=kOutput, calls=%fused_computation.31 | convolution fusion | flops 4831838208 | bytes 15073280 | tf_op jit(solution)/shard_map/dot_general | solution.py:64
  557.6 61.6 %all-reduce.19.cloned.1.call-done = f32[4096,128]{1,0:T(8,128)} async-done(((f32[4096,128]{1,0:T(8,128)}), f32[4096,128]{1,0:T(8,128)}) %all-reduce.19.cloned.1.call-update) | async-done | bytes 2097168 | tf_op jit(solution)/shard_map/psum | solution.py:71
  619.2 2.3 dynamic-slice_select_fusion
  621.6 51.6 %all-reduce.21.cloned.1.call-done = f32[2048,128]{1,0:T(8,128)} async-done(((f32[2048,128]{1,0:T(8,128)}), f32[2048,128]{1,0:T(8,128)}) %all-reduce.21.cloned.1.call-update) | async-done | bytes 1048592 | tf_op jit(solution)/shard_map/psum | solution.py:11
  673.2 42.1 %convolution_bitcast_fusion = f32[4096,128]{0,1:T(8,128)} fusion(f32[2048,128]{1,0:T(8,128)} %all-reduce.21.cloned.1.call-done, f32[4096,2048]{1,0:T(8,128)} %param.10), kind=kOutput, calls=%fused_computation.2 | convolution fusion | flops 12884901888 | bytes 36700160 | tf_op jit(solution)/shard_map/dot_general | solution.py:74
  715.3 61.2 %all-reduce.23.cloned.1.call-done = f32[4096,128]{0,1:T(8,128)} async-done(((f32[4096,128]{0,1:T(8,128)}), f32[4096,128]{0,1:T(8,128)}) %all-reduce.23.cloned.1.call-update) | async-done | bytes 2097168 | tf_op jit(solution)/shard_map/psum | solution.py:77
  776.5 4.0 multiply_subtract_fusion
  780.5 2.9 copy.9
  (39 shorter events, 1.0 us)
Async XLA Ops:
  7.2 1.1 copy-start
  7.2 5.7 copy-start.5
  7.2 83.8 %reduce-scatter.2.cloned.1.call-start = ((), (), s32[]{:S(2)}) async-start(), calls=%async_computation.1 | async-start | bytes 2949120 | tf_op jit(solution)/shard_map/reduce_scatter | solution.py:33
  12.8 134.6 %all-gather.2.cloned.1.call-start = ((), (), s32[]{:S(2)}) async-start(), calls=%async_computation.2 | async-start | bytes 2949120 | tf_op jit(solution)/shard_map/all_gather | solution.py:39
  12.9 35.8 %collective-permute-start = (f32[4096,96]{0,1:T(8,128)S(1)}, f32[4096,96]{0,1:T(8,128)S(1)}, u32[]{:S(2)}, u32[]{:S(2)}) collective-permute-start(f32[4096,96]{0,1:T(8,128)S(1)} %copy-done.5), channel_id=1, source_target_pairs={{0,4},{4,8},{8,12},{12,16},{16,20},{20,24},{24,28},{28,0},{1,5},{5... | collective-permute-start | bytes 4718600 | tf_op jit(solution)/shard_map/ppermute | solution.py:23
  13.4 36.7 %collective-permute-start.1 = (f32[4096,96]{0,1:T(8,128)S(1)}, f32[4096,96]{0,1:T(8,128)}, u32[]{:S(2)}, u32[]{:S(2)}) collective-permute-start(f32[4096,96]{0,1:T(8,128)S(1)} %copy-done.5), channel_id=1, source_target_pairs={{0,28},{4,0},{8,4},{12,8},{16,12},{20,16},{24,20},{28,24},{1,29},{... | collective-permute-start | bytes 4718600 | tf_op jit(solution)/shard_map/ppermute | solution.py:26
  48.6 1.4 copy-start.6
  48.7 34.9 %collective-permute-start.2 = (f32[4096,96]{0,1:T(8,128)S(1)}, f32[4096,96]{0,1:T(8,128)}, u32[]{:S(2)}, u32[]{:S(2)}) collective-permute-start(f32[4096,96]{0,1:T(8,128)S(1)} %collective-permute-done), channel_id=1, source_target_pairs={{0,4},{4,8},{8,12},{12,16},{16,20},{20,24},{24,28},{28,0},{1,5},{5... | collective-permute-start | bytes 4718600 | tf_op jit(solution)/shard_map/ppermute | solution.py:23
  50.1 43.6 %collective-permute-start.3 = (f32[4096,96]{0,1:T(8,128)}, f32[4096,96]{0,1:T(8,128)}, u32[]{:S(2)}, u32[]{:S(2)}) collective-permute-start(f32[4096,96]{0,1:T(8,128)} %collective-permute-done.1), channel_id=1, source_target_pairs={{0,28},{4,0},{8,4},{12,8},{16,12},{20,16},{24,20},{28,24},{1,29},{... | collective-permute-start | bytes 4718600 | tf_op jit(solution)/shard_map/ppermute | solution.py:26
  83.6 27.1 %collective-permute-start.4 = (f32[4096,96]{0,1:T(8,128)}, f32[4096,96]{0,1:T(8,128)}, u32[]{:S(2)}, u32[]{:S(2)}) collective-permute-start(f32[4096,96]{0,1:T(8,128)} %collective-permute-done.2), channel_id=1, source_target_pairs={{0,4},{4,8},{8,12},{12,16},{16,20},{20,24},{24,28},{28,0},{1,5},{5... | collective-permute-start | bytes 4718600 | tf_op jit(solution)/shard_map/ppermute | solution.py:23
  91.0 148.5 %all-reduce.9.cloned.1.call-start = ((), (), s32[]{:S(2)}) async-start(), calls=%async_computation.3 | async-start | bytes 786432 | tf_op jit(solution)/shard_map/psum | solution.py:62
  93.7 34.0 %collective-permute-start.5 = (f32[4096,96]{0,1:T(8,128)}, f32[4096,96]{0,1:T(8,128)S(1)}, u32[]{:S(2)}, u32[]{:S(2)}) collective-permute-start(f32[4096,96]{0,1:T(8,128)} %collective-permute-done.3), channel_id=1, source_target_pairs={{0,28},{4,0},{8,4},{12,8},{16,12},{20,16},{24,20},{28,24},{1,29},{... | collective-permute-start | bytes 4718600 | tf_op jit(solution)/shard_map/ppermute | solution.py:26
  110.7 27.6 %collective-permute-start.6 = (f32[4096,96]{0,1:T(8,128)}, f32[4096,96]{0,1:T(8,128)S(1)}, u32[]{:S(2)}, u32[]{:S(2)}) collective-permute-start(f32[4096,96]{0,1:T(8,128)} %collective-permute-done.4), channel_id=1, source_target_pairs={{0,4},{4,8},{8,12},{12,16},{16,20},{20,24},{24,28},{28,0},{1,5},{5... | collective-permute-start | bytes 4718600 | tf_op jit(solution)/shard_map/ppermute | solution.py:23
  147.4 2.4 copy-start.4
  149.8 39.1 %copy-start.3 = (f32[4096,128]{1,0:T(8,128)S(1)}, f32[4096,128]{1,0:T(8,128)}, u32[]{:S(2)}) copy-start(f32[4096,128]{1,0:T(8,128)} %param.9) | copy-start | bytes 6291460
  184.3 4.5 copy-start.2
  188.8 50.7 %copy-start.7 = (s32[768,128]{1,0:T(8,128)S(1)}, s32[768,128]{1,0:T(8,128)}, u32[]{:S(2)}) copy-start(s32[768,128]{1,0:T(8,128)} %param.11) | copy-start | bytes 1179652
  199.5 125.5 %all-reduce.11.cloned.1.call-start = ((), (), s32[]{:S(2)}) async-start(), calls=%async_computation.4 | async-start | bytes 4194304 | tf_op jit(solution)/shard_map/psum | solution.py:71
  263.4 115.4 %all-reduce.13.cloned.1.call-start = ((), (), s32[]{:S(2)}) async-start(), calls=%async_computation.5 | async-start | bytes 2097152 | tf_op jit(solution)/shard_map/psum | solution.py:11
  327.3 155.2 %all-reduce.15.cloned.1.call-start = ((), (), s32[]{:S(2)}) async-start(), calls=%async_computation.6 | async-start | bytes 4194304 | tf_op jit(solution)/shard_map/psum | solution.py:77
  421.3 111.3 %all-reduce.17.cloned.1.call-start = ((), (), s32[]{:S(2)}) async-start(), calls=%async_computation.7 | async-start | bytes 786432 | tf_op jit(solution)/shard_map/psum | solution.py:62
  496.4 122.8 %all-reduce.19.cloned.1.call-start = ((), (), s32[]{:S(2)}) async-start(), calls=%async_computation.8 | async-start | bytes 4194304 | tf_op jit(solution)/shard_map/psum | solution.py:71
  533.7 23.8 %copy-start.8 = (f32[768,128]{1,0:T(8,128)}, f32[768,128]{1,0:T(8,128)S(1)}, u32[]{:S(2)}) copy-start(f32[768,128]{1,0:T(8,128)S(1)} %divide_subtract_fusion) | copy-start | bytes 1179652
  557.5 115.6 %all-reduce.21.cloned.1.call-start = ((), (), s32[]{:S(2)}) async-start(), calls=%async_computation.9 | async-start | bytes 2097152 | tf_op jit(solution)/shard_map/psum | solution.py:11
  621.5 154.9 %all-reduce.23.cloned.1.call-start = ((), (), s32[]{:S(2)}) async-start(), calls=%async_computation.10 | async-start | bytes 4194304 | tf_op jit(solution)/shard_map/psum | solution.py:77
  776.5 6.9 copy-start.1
Sparse Core Ops, SparseCore 0:
  12.9 50.4 reduce-scatter.1
  91.1 56.2 all-gather.1
  199.6 39.8 all-reduce.8
  263.5 61.4 all-reduce.10
  327.8 50.9 all-reduce.12
  421.4 61.0 all-reduce.14
  496.5 36.0 all-reduce.16
  557.7 61.5 all-reduce.18
  622.2 50.9 all-reduce.20
  715.4 61.0 all-reduce.22
